TPU v7x, 512 devices: a whole 4x8x8 slice. The times are simulated.
512 devices in a mesh: group: 32 (over x, y_lo, core), pos: 16 (over z, y_hi).
Axes of the slice: x: 4, y: 8 (y_hi: 2, y_lo: 4; y = y_hi * 4 + y_lo), z: 8, core: 2. Of those that a mesh axis runs over, the one named last changes fastest.
Arguments:
- potential: float32 [4, 2, 6144, 2048], P(None, None, 'group', 'pos'), may hold values from -0.3 to 0.3
- probe: float32 [32, 4, 128, 256], P('group', None, 'pos'), may hold values from -3 to 3
- amplitudes: bfloat16 [32, 16, 3, 128, 128], P('group', 'pos'), may hold values from 0.1 to 8, as said below
- row_offset: int32 [32, 16, 3], P('group', 'pos'), may hold values from 0 to 64
- col_offset: int32 [32, 16, 3], P('group', 'pos'), may hold values from 0 to 127
- counts: int32 [32, 16], P('group', 'pos'), may hold values from 1 to 3, as said below
Outputs:
- object_grad: float32 [4, 2, 6144, 2048], P(None, None, 'group', 'pos')
- probe_grad: float32 [32, 4, 128, 256], P('group', None, 'pos')
Inputs may be any that keep to these rules, and one draw needn't show every extreme that they name: A tile's positions fill its first counts slots and later slots are unused; at least one tile has 3. `amplitudes`: every entry is positive.
All inputs are finite; a program needn't handle non-finite values.
Results may differ from a plain program's by a relative error of at most 0.02.
The roundings to bfloat16 on the way count: a program that leaves them out, or rounds other values in their place, can miss the bound.
Values sent between devices are 32-bit elements; how exact they have to be, the bound alone decides.
A program may use at most 64 MiB of HBM per device.

v0:
```python
import math

import jax
import jax.numpy as jnp
from jax import lax
from jax.sharding import PartitionSpec as P

PROP = 0.25
REG = 0.1


def shifted(block, axis, distance):
    devices = range(lax.axis_size(axis))
    route = [(i - distance, i) for i in devices if i - distance in devices]
    return lax.ppermute(block, axis, route)


def tables(size):
    idx = jnp.arange(size, dtype=jnp.int32)
    prod = idx[:, None] * idx[None, :] % size
    angle = 2.0 * math.pi / size * prod.astype(jnp.float32)
    cosv = jnp.cos(angle) / math.sqrt(size)
    sinv = jnp.sin(angle) / math.sqrt(size)
    forward = jnp.concatenate(
        [jnp.concatenate([cosv, -sinv], 1), jnp.concatenate([sinv, cosv], 1)], 0
    )
    inverse = jnp.concatenate(
        [jnp.concatenate([cosv, sinv], 1), jnp.concatenate([-sinv, cosv], 1)], 0
    )
    return (forward.astype(jnp.bfloat16), inverse.astype(jnp.bfloat16))


def propagator(size):
    idx = jnp.arange(size, dtype=jnp.int32)
    freq = jnp.where(idx < size // 2, idx, idx - size).astype(jnp.float32)
    phase = (
        -2.0
        * math.pi
        * PROP
        / size
        * (freq[:, None] * freq[:, None] + freq[None, :] * freq[None, :])
    )
    return jnp.concatenate([jnp.cos(phase), jnp.sin(phase)], 1)


def along_last(wave, table):
    size = wave.shape[-2]
    flat = wave.reshape(-1, 2 * size).astype(jnp.bfloat16)
    return jnp.dot(flat, table, preferred_element_type=jnp.float32).reshape(wave.shape)


def flip(wave):
    lead = wave.shape[:-2]
    size = wave.shape[-2]
    parts = wave.reshape(lead + (size, 2, size))
    return jnp.swapaxes(parts, -3, -1).reshape(lead + (size, 2 * size))


def transform(wave, table):
    return flip(along_last(flip(along_last(wave, table)), table))


def cmul(left, right):
    size = left.shape[-2]
    lre, lim = (left[..., :size], left[..., size:])
    rre, rim = (right[..., :size], right[..., size:])
    return jnp.concatenate([lre * rre - lim * rim, lre * rim + lim * rre], -1)


def cmulc(left, right):
    size = left.shape[-2]
    lre, lim = (left[..., :size], left[..., size:])
    rre, rim = (right[..., :size], right[..., size:])
    return jnp.concatenate([lre * rre + lim * rim, lre * rim - lim * rre], -1)


def transmit(patch):
    magnitude = jnp.exp(-patch[:, 1])
    return jnp.concatenate([magnitude * jnp.cos(patch[:, 0]), magnitude * jnp.sin(patch[:, 0])], -1)


def potential_grad(trans, tgrad):
    size = trans.shape[-2]
    quot = cmulc(trans, tgrad)
    return jnp.stack([quot[:, size:], -quot[:, :size]], 0)


def one_position(carry, extended, whole, observed, row, col, weight, forward, inverse, kernel):
    grad_ext, probe_acc, misfit = carry
    slices = extended.shape[0]
    size = whole.shape[-2]
    zero = jnp.zeros((), jnp.int32)
    start = (zero, zero, row, col)
    patch = lax.dynamic_slice(extended, start, (slices, 2, size, size))
    trans = transmit(patch)
    psi = whole
    stored = []
    exit_wave = psi
    for layer in range(slices):
        stored.append(psi)
        exit_wave = cmul(trans[layer][None], psi)
        if layer + 1 < slices:
            psi = transform(cmul(kernel[None], transform(exit_wave, forward)), inverse)
    far = transform(exit_wave, forward)
    real_part, imag_part = (far[..., :size], far[..., size:])
    inten = jnp.sum(real_part * real_part + imag_part * imag_part, axis=0)
    model = jnp.sqrt(inten + REG)
    diff = model - observed
    misfit = misfit + weight * jnp.sum(diff * diff)
    ratio = weight * (1.0 - observed / model)
    wave_grad = transform(far * jnp.concatenate([ratio, ratio], -1)[None], inverse)
    pieces = [None] * slices
    psi_grad = wave_grad
    for layer in reversed(range(slices)):
        tgrad = jnp.sum(cmulc(stored[layer], wave_grad), axis=0)
        pieces[layer] = potential_grad(trans[layer], tgrad)
        psi_grad = cmulc(trans[layer][None], wave_grad)
        if layer > 0:
            wave_grad = transform(cmulc(kernel[None], transform(psi_grad, forward)), inverse)
    block = jnp.stack(pieces, 0)
    old = lax.dynamic_slice(grad_ext, start, block.shape)
    grad_ext = lax.dynamic_update_slice(grad_ext, old + block, start)
    return (grad_ext, probe_acc + psi_grad, misfit)


def body(potential, probe, amplitudes, row_offset, col_offset, counts):
    slices = potential.shape[0]
    rows_tile = potential.shape[2]
    size = potential.shape[3]
    forward, inverse = tables(size)
    kernel = propagator(size)
    neighbour = shifted(potential, "pos", -1)
    extended = jnp.concatenate([potential, neighbour], 3)
    whole = lax.all_gather(probe, "pos", axis=2, tiled=True)[0]
    amps = amplitudes[0, 0].astype(jnp.float32)
    rows_here = row_offset[0, 0]
    cols_here = col_offset[0, 0]
    count = counts[0, 0]
    slots = amps.shape[0]

    def slot_step(slot, inner):
        weight = (slot < count).astype(jnp.float32)
        return one_position(
            inner,
            extended,
            whole,
            amps[slot],
            rows_here[slot],
            cols_here[slot],
            weight,
            forward,
            inverse,
            kernel,
        )

    init = (
        jnp.zeros((slices, 2, rows_tile, 2 * size), jnp.float32),
        jnp.zeros(whole.shape, jnp.float32),
        jnp.zeros((), jnp.float32),
    )
    grad_ext, probe_acc, misfit = lax.fori_loop(0, slots, slot_step, init)
    arrived = shifted(grad_ext[..., size:], "pos", 1)
    grad_own = grad_ext[..., :size] + arrived
    misfit_all, total = lax.psum((misfit, count.astype(jnp.float32)), ("group", "pos"))
    scale = 1.0 / jnp.sqrt(misfit_all / (total * size * size) + 1e-06)
    summed = lax.psum(probe_acc, "pos")
    own_rows = probe.shape[2]
    begin = lax.axis_index("pos") * own_rows
    share = lax.dynamic_slice_in_dim(summed, begin, own_rows, 1)
    return (grad_own * scale, (share * scale)[None])


def solution(mesh):
    placed = (
        P(None, None, "group", "pos"),
        P("group", None, "pos", None),
        P("group", "pos", None, None, None),
        P("group", "pos", None),
        P("group", "pos", None),
        P("group", "pos"),
    )
    return jax.shard_map(
        body,
        mesh=mesh,
        in_specs=placed,
        out_specs=(P(None, None, "group", "pos"), P("group", None, "pos", None)),
        check_vma=False,
    )
```

profile of v0, /device:TPU:2, one launch (start us, length us, event | category | flops | bytes accessed | tf_op | source)
XLA Modules:
  0.0 466.3 jit_solution(10442040989172087452)
XLA Ops:
  7.2 1.3 copy.41
  8.5 1.3 collective-permute-start
  11.5 0.7 bitcast_convert_fusion
  12.2 96.1 %all_gather.3 = f32[1,4,128,256]{3,2,1,0:T(8,128)S(1)} all-gather(f32[1,4,8,256]{3,2,1,0:T(8,128)} %param.9), channel_id=1, replica_groups=mesh['group'=32,'pos'=16] {'pos'}, dimensions={2}, use_global_device_ids=true | all-gather | bytes 557056 | tf_op jit(solution)/shard_map/all_gather | solution.py:134
  108.3 1.3 pad_maximum_fusion.2
  109.6 1.3 broadcast_in_dim.14
  110.9 125.7 %while.18 = (s32[]{:T(128)}, f32[4,2,192,256]{3,2,1,0:T(8,128)}, f32[4,128,256]{2,1,0:T(8,128)}, f32[]{:T(128)}, s32[3]{0:T(128)S(1)}, /*index=5*/s32[3]{0:T(128...) while((s32[]{:T(128)}, f32[4,2,192,256]{3,2,1,0:T(8,128)}, ...), condition=%wide.region_7.8_spmd.clone, body=%wide.region_0.7_spmd.clone.sunk | while | flops 1899905024 | bytes 103744496 | solution.py:161
  116.4 0.9 slice_bitcast_fusion.13
  117.3 2.2 cosine_multiply_fusion.2
  126.7 1.5 fusion.287
  128.8 0.9 fusion.270
  130.4 0.7 fusion.273
  131.2 1.1 copy.177
  132.3 1.0 add_convert_fusion.19
  136.3 0.7 maximum_reduce_fusion.9
  139.2 0.7 maximum_reduce_fusion.10
  142.1 0.8 copy-done.3
  145.1 6.8 %dynamic_update_slice.9 = f32[4,2,192,256]{3,2,1,0:T(8,128)S(1)} dynamic-update-slice(f32[4,2,192,256]{3,2,1,0:T(8,128)S(1)} %copy-done, f32[4,2,128,128]{3,2,1,0:T(8,128)S(1)} %maximum_add_fusion.4, s32[]{:T(128)} %constant.87.clone.1..sunk, s32[]{:T(128)} %constant.87.clone.1..sunk, s32[]{:T(128)S(6)} %select_n.86, s32[]{:T(128)S(6)} %select_n.87) | dynamic-update-slice | bytes 1048580 | tf_op jit(solution)/shard_map/while/body/eval_jaxpr/dynamic_update_slice | solution.py:122
  151.9 1.1 copy-done.1
  158.6 0.9 slice_bitcast_fusion.13
  159.5 2.2 cosine_multiply_fusion.2
  168.8 1.5 fusion.287
  170.9 0.9 fusion.270
  172.5 0.7 fusion.273
  173.4 1.1 copy.177
  174.4 1.0 add_convert_fusion.19
  178.4 0.7 maximum_reduce_fusion.9
  181.3 0.7 maximum_reduce_fusion.10
  184.3 0.8 copy-done.3
  187.2 6.5 %dynamic_update_slice.9 = f32[4,2,192,256]{3,2,1,0:T(8,128)S(1)} dynamic-update-slice(f32[4,2,192,256]{3,2,1,0:T(8,128)S(1)} %copy-done, f32[4,2,128,128]{3,2,1,0:T(8,128)S(1)} %maximum_add_fusion.4, s32[]{:T(128)} %constant.87.clone.1..sunk, s32[]{:T(128)} %constant.87.clone.1..sunk, s32[]{:T(128)S(6)} %select_n.86, s32[]{:T(128)S(6)} %select_n.87) | dynamic-update-slice | bytes 1048580 | tf_op jit(solution)/shard_map/while/body/eval_jaxpr/dynamic_update_slice | solution.py:122
  193.7 1.1 copy-done.1
  200.4 0.9 slice_bitcast_fusion.13
  201.3 2.2 cosine_multiply_fusion.2
  210.6 1.5 fusion.287
  212.7 0.9 fusion.270
  214.3 0.7 fusion.273
  215.2 1.1 copy.177
  216.3 1.0 add_convert_fusion.19
  223.1 0.7 maximum_reduce_fusion.10
  226.1 0.8 copy-done.3
  229.0 6.4 %dynamic_update_slice.9 = f32[4,2,192,256]{3,2,1,0:T(8,128)S(1)} dynamic-update-slice(f32[4,2,192,256]{3,2,1,0:T(8,128)S(1)} %copy-done, f32[4,2,128,128]{3,2,1,0:T(8,128)S(1)} %maximum_add_fusion.4, s32[]{:T(128)} %constant.87.clone.1..sunk, s32[]{:T(128)} %constant.87.clone.1..sunk, s32[]{:T(128)S(6)} %select_n.86, s32[]{:T(128)S(6)} %select_n.87) | dynamic-update-slice | bytes 1048580 | tf_op jit(solution)/shard_map/while/body/eval_jaxpr/dynamic_update_slice | solution.py:122
  235.5 1.1 copy-done.1
  236.6 1.3 slice.508
  237.9 1.3 collective-permute-start.1
  240.0 126.4 %all-reduce = (f32[]{:T(128)}, f32[]{:T(128)}) all-reduce(f32[]{:T(128)} %get-tuple-element.219, f32[]{:T(128)S(6)} %convert_element_type.337), channel_id=1, replica_groups=mesh['group'=32,'pos'=16] {'group','pos'}, use_global_device_ids=true, to_apply=%region_8.9 | all-reduce | flops 2 | bytes 16 | tf_op jit(solution)/shard_map/psum | solution.py:164
  367.6 89.5 %all-reduce.3.cloned.1.call-done = f32[4,128,256]{2,1,0:T(8,128)} async-done(((f32[4,128,256]{2,1,0:T(8,128)}), f32[4,128,256]{2,1,0:T(8,128)}) %all-reduce.3.cloned.1.call-update) | async-done | bytes 524304 | tf_op jit(solution)/shard_map/psum | solution.py:166
  457.1 1.4 multiply_bitcast_fusion
  458.5 1.0 add_multiply_fusion
  (440 shorter events, 55.7 us)
Async XLA Ops:
  7.2 101.1 %copy-start.23 = (f32[4,2,192,128]{3,2,1,0:T(8,128)S(1)}, f32[4,2,192,128]{3,2,1,0:T(8,128)}, u32[]{:S(2)}) copy-start(f32[4,2,192,128]{3,2,1,0:T(8,128)} %param.8) | copy-start | bytes 2359300
  7.2 2.9 copy-start.24
  7.2 450.0 %all-reduce.3.cloned.1.call-start = ((), (), s32[]{:S(2)}) async-start(), calls=%async_computation | async-start | bytes 1048576 | tf_op jit(solution)/shard_map/psum | solution.py:166
  8.5 99.8 %collective-permute-start = (f32[4,2,192,128]{3,2,0,1:T(8,128)S(1)}, f32[4,2,192,128]{3,2,0,1:T(8,128)S(1)}, u32[]{:S(2)}, u32[]{:S(2)}) collective-permute-start(f32[4,2,192,128]{3,2,0,1:T(8,128)S(1)} %copy.41), channel_id=1, source_target_pairs={{1,0},{2,1},{3,2},{4,3},{5,4},{6,5},{7,6},{8,7},{9,8},{10,9},{11,1... | collective-permute-start | bytes 2359304 | tf_op jit(solution)/shard_map/ppermute | solution.py:15
  109.6 1.3 copy-start.25
  109.6 1.3 copy-start.26
  119.6 1.9 copy-start.9
  119.6 1.9 copy-start.11
  119.6 3.8 copy-start.13
  119.6 3.8 copy-start.15
  119.6 5.7 %copy-start.17 = (f32[128,128]{1,0:T(8,128)}, f32[128,128]{1,0:T(8,128)S(1)}, u32[]{:S(2)}) copy-start(f32[128,128]{1,0:T(8,128)S(1)} %get-tuple-element.594) | copy-start | bytes 196612 | tf_op jit(solution)/shard_map/while
  119.6 5.7 %copy-start.18 = (f32[128,128]{1,0:T(8,128)}, f32[128,128]{1,0:T(8,128)S(1)}, u32[]{:S(2)}) copy-start(f32[128,128]{1,0:T(8,128)S(1)} %get-tuple-element.595) | copy-start | bytes 196612 | tf_op jit(solution)/shard_map/while
  141.9 1.0 copy-start.3
  142.1 1.1 copy-start.20
  143.0 0.9 copy-start.21
  143.2 1.1 copy-start.4
  143.2 1.1 copy-start.22
  143.2 1.6 copy-start
  151.9 1.2 copy-start.1
  161.7 2.0 copy-start.9
  161.8 2.0 copy-start.11
  161.8 3.8 copy-start.13
  161.8 3.8 copy-start.15
  161.8 5.7 %copy-start.17 = (f32[128,128]{1,0:T(8,128)}, f32[128,128]{1,0:T(8,128)S(1)}, u32[]{:S(2)}) copy-start(f32[128,128]{1,0:T(8,128)S(1)} %get-tuple-element.594) | copy-start | bytes 196612 | tf_op jit(solution)/shard_map/while
  161.8 5.7 %copy-start.18 = (f32[128,128]{1,0:T(8,128)}, f32[128,128]{1,0:T(8,128)S(1)}, u32[]{:S(2)}) copy-start(f32[128,128]{1,0:T(8,128)S(1)} %get-tuple-element.595) | copy-start | bytes 196612 | tf_op jit(solution)/shard_map/while
  177.4 0.9 copy-start.16
  184.1 1.0 copy-start.3
  184.2 1.1 copy-start.20
  185.1 0.9 copy-start.21
  185.3 1.1 copy-start.4
  185.3 1.1 copy-start.22
  185.3 1.6 copy-start
  193.7 1.2 copy-start.1
  203.6 2.0 copy-start.9
  203.6 2.0 copy-start.11
  203.6 3.8 copy-start.13
  203.6 3.8 copy-start.15
  203.6 5.7 %copy-start.17 = (f32[128,128]{1,0:T(8,128)}, f32[128,128]{1,0:T(8,128)S(1)}, u32[]{:S(2)}) copy-start(f32[128,128]{1,0:T(8,128)S(1)} %get-tuple-element.594) | copy-start | bytes 196612 | tf_op jit(solution)/shard_map/while
  203.6 5.7 %copy-start.18 = (f32[128,128]{1,0:T(8,128)}, f32[128,128]{1,0:T(8,128)S(1)}, u32[]{:S(2)}) copy-start(f32[128,128]{1,0:T(8,128)S(1)} %get-tuple-element.595) | copy-start | bytes 196612 | tf_op jit(solution)/shard_map/while
  225.9 1.0 copy-start.3
  226.0 1.1 copy-start.20
  226.9 0.9 copy-start.21
  227.1 1.1 copy-start.4
  227.1 1.1 copy-start.22
  227.2 1.6 copy-start
  235.5 1.2 copy-start.1
  236.6 221.9 %copy-start.2 = (f32[4,2,192,256]{3,2,1,0:T(8,128)S(1)}, f32[4,2,192,256]{3,2,1,0:T(8,128)}, u32[]{:S(2)}) copy-start(f32[4,2,192,256]{3,2,1,0:T(8,128)} %get-tuple-element.218) | copy-start | bytes 4718596
  237.9 220.6 %collective-permute-start.1 = (f32[4,2,192,128]{3,2,1,0:T(8,128)S(1)}, f32[4,2,192,128]{3,2,1,0:T(8,128)S(1)}, u32[]{:S(2)}, u32[]{:S(2)}) collective-permute-start(f32[4,2,192,128]{3,2,1,0:T(8,128)S(1)} %slice.508), channel_id=1, source_target_pairs={{0,1},{1,2},{2,3},{3,4},{4,5},{5,6},{6,7},{7,8},{8,9},{9,10},{10,1... | collective-permute-start | bytes 2359304 | tf_op jit(solution)/shard_map/ppermute | solution.py:15
  (26 other events, 20.5 us)
Sparse Core Ops, SparseCore 0:
  239.4 217.6 all-reduce.2
where the time goes:
time: 468 us; the launch traced here: 466 us
  blocking collectives  222 us (47%)
  waiting for transfers between devices  89.5 us (19%)
  local copies, waits for them, and re-layouts  61.2 us (13%)
  other arithmetic  34.4 us (7%)
  matrix products  22.3 us (5%)
  loops' own time  17.7 us (4%)
  between operations  16.1 us (3%)
    psum x1, blocking collectives, body(): lax.psum((misfit, count.astype(jnp.float32)), ('group', 'pos'))  126 us
    all_gather x1, blocking collectives, body(): whole = lax.all_gather(probe, 'pos', axis=2, tiled=True)[0]  96.1 us
    psum x1, waiting for transfers between devices, body(): summed = lax.psum(probe_acc, 'pos')  89.5 us
    while x210, local copies, waits for them, and re-layouts  27.5 us
    dot_general x84, matrix products, along_last(): jnp.dot(flat, table, preferred_element_type=jnp.float32).reshape(wave.shape)  22.3 us
    dynamic_update_slice x3, local copies, waits for them, and re-layouts, one_position(): grad_ext = lax.dynamic_update_slice(grad_ext, old + block, start)  19.7 us
    another operation x1, loops' own time, body(): grad_ext, probe_acc, misfit = lax.fori_loop(0, slots, slot_step, init)  17.7 us
  transfers between devices with their start and end apart: 3, of which 1 were waited for; matrix products, arithmetic and copies ran while one was open for 1% of the time, Pallas kernels for 0%

commit v1 on v0

v1 whole, which is shorter than its diff:
```python
import math

import jax
import jax.numpy as jnp
import numpy as np
from jax import lax
from jax.experimental import pallas as pl
from jax.experimental.pallas import tpu as pltpu
from jax.sharding import PartitionSpec as P

PROP = 0.25
REG = 0.1
N = 128
MODES = 4
SLICES = 4
SLOTS = 3
ROWS = 192
XS, YL, ZS = 4, 4, 8
F32 = jnp.float32
BF16 = jnp.bfloat16


def tables():
    idx = np.arange(N, dtype=np.int32)
    prod = (idx[:, None] * idx[None, :] % N).astype(np.float32)
    angle = np.float32(2.0 * math.pi / N) * prod
    root = np.float32(math.sqrt(N))
    cosv = np.cos(angle.astype(np.float64)).astype(np.float32) / root
    sinv = np.sin(angle.astype(np.float64)).astype(np.float32) / root
    forward = np.concatenate([np.concatenate([cosv, -sinv], 1), np.concatenate([sinv, cosv], 1)], 0)
    inverse = np.concatenate([np.concatenate([cosv, sinv], 1), np.concatenate([-sinv, cosv], 1)], 0)
    return jnp.asarray(forward).astype(BF16), jnp.asarray(inverse).astype(BF16)


def propagator():
    idx = np.arange(N, dtype=np.int32)
    freq = np.where(idx < N // 2, idx, idx - N).astype(np.float32)
    factor = np.float32(-2.0 * math.pi * PROP / N)
    phase = factor * (freq[:, None] * freq[:, None] + freq[None, :] * freq[None, :])
    phase = phase.astype(np.float32).astype(np.float64)
    return jnp.asarray(np.concatenate([np.cos(phase), np.sin(phase)], 1).astype(np.float32))


def cmul(a, b):
    return a[0] * b[0] - a[1] * b[1], a[0] * b[1] + a[1] * b[0]


def cmulc(a, b):
    return a[0] * b[0] + a[1] * b[1], a[0] * b[1] - a[1] * b[0]


def dft(waves, right, left):
    rows = [jnp.concatenate([re.astype(BF16), im.astype(BF16)], 1) for re, im in waves]
    first = jnp.dot(jnp.concatenate(rows, 0), right, preferred_element_type=F32).astype(BF16)
    cols = []
    for m in range(len(waves)):
        part = first[m * N : (m + 1) * N]
        cols.append(jnp.concatenate([part[:, :N], part[:, N:]], 0))
    second = jnp.dot(left, jnp.concatenate(cols, 1), preferred_element_type=F32)
    return [(second[:N, m * N : (m + 1) * N], second[N:, m * N : (m + 1) * N]) for m in range(len(waves))]


def kernel(
    pot, probe, amps_in, row_in, col_in, cnt_in, fwd_in, inv_in, kern_in,
    out_obj, out_probe,
    n0, n1, n2, n3, c0, c1, c2, c3, gn, gc, rbuf, xbuf, sbuf, amps, amps_out, metav, meta_out, meta,
    pbuf, psi0, psi, wav, tr, gp, pacc, pgr, px, pzr, pown, pfin,
    mis, misr, smis,
    loc_sem, s_misc, r_probe, r_meta, r_amp,
    s_n, r_n, s_c, r_c, s_f, r_f, s_pz, r_pz, s_pf, r_pf,
    s_x, r_x, s_r, r_r, s_rn, r_rn, s_px, r_px, s_pq, r_pq, s_po, r_po, s_m, r_m,
):
    nbuf = (n0, n1, n2, n3)
    cbuf = (c0, c1, c2, c3)
    g = lax.axis_index("group")
    pos = lax.axis_index("pos")
    x, yl, c = g // 8, (g // 2) % 4, g % 2
    z, h = pos // 2, pos % 2
    oh = 1 - h
    oc = 1 - c
    nat = c == h
    guest = c != h
    keep = jnp.where(nat, 0, 1)
    give = 1 - keep
    dz = jnp.where(h == 0, ZS - 1, 1)

    def dev(xx, yy, hh, zz, cc):
        return {"group": xx * 8 + yy * 2 + cc, "pos": zz * 2 + hh}

    def remote(src, dst, send, recv, to):
        return pltpu.make_async_remote_copy(src_ref=src, dst_ref=dst, send_sem=send, recv_sem=recv, device_id=to)

    def at_z(k):
        return lax.rem(z + k, ZS)

    sibling = dev(x, yl, h, z, oc)
    ring_z = [dev(x, yl, h, at_z(k), c) for k in range(1, ZS)]
    ring_y = []
    for k in range(1, 8):
        y = lax.rem(h * 4 + yl + k, 8)
        ring_y.append(dev(x, y % 4, y // 4, z, c))
    ring_x = []
    for k in range(1, 8):
        q = lax.rem(x * 2 + c + k, 8)
        ring_x.append(dev(q // 2, yl, h, z, q % 2))
    partners = ring_z + ring_y + ring_x
    partners += [dev(x, yl, oh, z, oc), dev(x, yl, h, at_z(1), oc), dev(x, yl, h, at_z(ZS - 1), oc)]

    barrier = pltpu.get_barrier_semaphore()
    for partner in partners:
        pl.semaphore_signal(barrier, inc=1, device_id=partner)

    lane = lax.broadcasted_iota(jnp.int32, (8, N), 1)
    packed = jnp.zeros((8, N), jnp.int32)
    for p in range(SLOTS):
        packed = jnp.where(lane == p, row_in[0, 0, p], packed)
        packed = jnp.where(lane == SLOTS + p, col_in[0, 0, p], packed)
    packed = jnp.where(lane == 2 * SLOTS, cnt_in[0, 0], packed)
    meta_out[...] = packed
    for p in range(SLOTS):
        amps_out[p] = amps_in[0, 0, p].astype(F32)
    gp[...] = jnp.zeros_like(gp)

    pl.semaphore_wait(barrier, len(partners))

    to_probe = remote(probe.at[0], pbuf.at[h, z], s_misc.at[0], r_probe, dev(x, yl, oh, z, oc))
    to_meta = remote(meta_out, metav, s_misc.at[1], r_meta, dev(x, yl, oh, z, 1))
    to_amp = remote(amps_out, amps, s_misc.at[2], r_amp, dev(x, yl, oh, z, 1))
    to_metan = remote(meta_out, metav, s_misc.at[1], r_meta, dev(x, yl, h, at_z(1), 0))
    to_ampn = remote(amps_out, amps, s_misc.at[2], r_amp, dev(x, yl, h, at_z(1), 0))
    to_n = [remote(pot.at[s], nbuf[s], s_n.at[s], r_n.at[s], dev(x, yl, h, lax.rem(z + dz, ZS), oc)) for s in range(SLICES)]
    to_c = [
        [remote(pot.at[s, ch], cbuf[s].at[ch], s_c.at[s, ch], r_c.at[s], dev(x, yl, oh, z, c if ch == 0 else oc)) for ch in range(2)]
        for s in range(SLICES)
    ]
    own_probe = [remote(probe.at[0], pbuf.at[c, z], s_pz.at[k], r_pz.at[k], ring_z[k]) for k in range(ZS - 1)]
    got_probe = [remote(pbuf.at[c, z], pbuf.at[c, z], s_pz.at[k], r_pz.at[k], ring_z[k]) for k in range(ZS - 1)]
    loc_n = [pltpu.make_async_copy(pot.at[s], nbuf[s], loc_sem.at[s]) for s in range(SLICES)]
    loc_p = pltpu.make_async_copy(probe.at[0], pbuf.at[c, z], loc_sem.at[4])
    loc_a = pltpu.make_async_copy(amps_out, amps, loc_sem.at[5])
    loc_m = pltpu.make_async_copy(meta_out, metav, loc_sem.at[6])
    loc_s = pltpu.make_async_copy(metav, meta, loc_sem.at[7])
    here = jnp.logical_and(nat, h == 0)
    along = jnp.logical_and(nat, h == 1)

    @pl.when(guest)
    def _():
        to_probe.start()
        to_meta.start()
        for s in range(SLICES):
            for ch in range(2):
                to_c[s][ch].start()
        to_amp.start()

    @pl.when(nat)
    def _():
        for k in (0, 6, 1, 5, 2, 4, 3):
            own_probe[k].start()
        loc_p.start()
        for s in range(SLICES):
            loc_n[s].start()

    @pl.when(along)
    def _():
        to_metan.start()

    @pl.when(here)
    def _():
        loc_a.start()
        loc_m.start()

    @pl.when(nat)
    def _():
        for s in range(SLICES):
            to_n[s].start()

    @pl.when(along)
    def _():
        to_ampn.start()

    @pl.when(here)
    def _():
        loc_m.wait()

    @pl.when(jnp.logical_not(here))
    def _():
        to_meta.wait_recv()

    loc_s.start()

    @pl.when(guest)
    def _():
        to_probe.wait_recv()
        for k in (0, 6, 1, 5, 2, 4, 3):
            got_probe[k].start()

    @pl.when(nat)
    def _():
        loc_p.wait()

    loc_s.wait()

    fwd_c = [remote(cbuf[s].at[keep], cbuf[s].at[keep], s_f.at[s], r_f.at[s], sibling) for s in range(SLICES)]
    got_c = [remote(cbuf[s].at[keep], cbuf[s].at[keep], s_f.at[s], r_c.at[s], sibling) for s in range(SLICES)]

    def pass_on(s):
        got_c[s].wait_recv()
        fwd_c[s].start()

    last = jnp.logical_or(
        jnp.logical_and(jnp.logical_and(h == 0, c == 1), z == ZS - 1),
        jnp.logical_and(jnp.logical_and(h == 1, c == 0), z == 0),
    )
    alive = jnp.where(last, 0, 1)

    def masks(p, rows):
        col = meta[0, SLOTS + p]
        spot = lax.broadcasted_iota(jnp.int32, (rows, N), 1)
        n_lo = jnp.where(c == 0, col, 0)
        n_hi = jnp.where(c == 0, N, col * alive)
        c_lo = jnp.where(c == 0, 0, col)
        c_hi = jnp.where(c == 0, col * alive, N)
        in_n = jnp.logical_and(spot >= n_lo, spot < n_hi)
        in_c = jnp.logical_and(spot >= c_lo, spot < c_hi)
        return in_n, in_c, col

    def transmit(s):
        @pl.when(nat)
        def _():
            loc_n[s].wait()

        @pl.when(guest)
        def _():
            to_n[s].wait_recv()

        fwd_c[s].wait_recv()

        def one(p, carry):
            in_n, in_c, col = masks(p, N)
            row = meta[0, p]
            shift = lax.rem(N - col, N)
            parts = []
            for ch in range(2):
                near = nbuf[s][ch, pl.ds(row, N), :]
                far = cbuf[s][ch, pl.ds(row, N), :]
                both = jnp.where(in_n, near, jnp.where(in_c, far, 0.0))
                parts.append(pltpu.roll(both, shift, 1))
            mag = jnp.exp(-parts[1])
            tr[s, p, 0] = mag * jnp.cos(parts[0])
            tr[s, p, 1] = mag * jnp.sin(parts[0])
            return carry

        lax.fori_loop(0, SLOTS, one, 0)

    def pair(ref, *at):
        return ref[(*at, slice(None), slice(0, N))], ref[(*at, slice(None), slice(N, 2 * N))]

    def put(ref, value, *at):
        ref[(*at, slice(None), slice(0, N))] = value[0]
        ref[(*at, slice(None), slice(N, 2 * N))] = value[1]

    def psi_at(s, p, m):
        return pair(psi0, m) if s == 0 else pair(psi, s - 1, p, m)

    def trans_at(s, p):
        return tr[s, p, 0], tr[s, p, 1]

    def prop(s):
        def one(p, carry):
            t = trans_at(s, p)
            kern = pair(kern_in)
            waves = dft([cmul(t, psi_at(s, p, m)) for m in range(MODES)], fwd_in[...], inv_in[...])
            waves = dft([cmul(kern, w) for w in waves], inv_in[...], fwd_in[...])
            for m in range(MODES):
                put(psi, waves[m], s, p, m)
            return carry

        lax.fori_loop(0, SLOTS, one, 0)

    pass_on(0)
    transmit(0)
    for k in range(ZS - 1):
        own_probe[k].wait_recv()
    fwd_p = remote(pbuf.at[c], pbuf.at[c], s_pf, r_pf, sibling)
    fwd_p.start()
    pass_on(1)
    fwd_p.wait_recv()
    for zz in range(ZS):
        for hh in range(2):
            at = (2 * zz + hh) * 8
            for m in range(MODES):
                psi0[m, at : at + 8, :] = pbuf[hh, zz, m]
    prop(0)
    pass_on(2)
    transmit(1)
    prop(1)
    pass_on(3)
    transmit(2)
    prop(2)
    transmit(3)

    @pl.when(here)
    def _():
        loc_a.wait()

    @pl.when(jnp.logical_not(here))
    def _():
        to_amp.wait_recv()

    count = meta[0, 2 * SLOTS]
    mis[0:8, :] = jnp.zeros((8, N), F32)
    mis[8:16, :] = jnp.zeros((8, N), F32) + count.astype(F32)

    def detect(p, carry):
        weight = jnp.where(p < count, 1.0, 0.0)
        t = trans_at(SLICES - 1, p)
        far = dft([cmul(t, psi_at(SLICES - 1, p, m)) for m in range(MODES)], fwd_in[...], inv_in[...])
        inten = far[0][0] * far[0][0] + far[0][1] * far[0][1]
        for m in range(1, MODES):
            inten = inten + (far[m][0] * far[m][0] + far[m][1] * far[m][1])
        model = jnp.sqrt(inten + REG)
        seen = amps[p]
        diff = model - seen
        sq = weight * (diff * diff)
        part = sq[0:8]
        for r in range(1, N // 8):
            part = part + sq[r * 8 : r * 8 + 8]
        mis[0:8, :] = mis[0:8, :] + part
        ratio = weight * (1.0 - seen / model)
        waves = dft([(w[0] * ratio, w[1] * ratio) for w in far], inv_in[...], fwd_in[...])
        for m in range(MODES):
            put(wav, waves[m], p, m)
        return carry

    lax.fori_loop(0, SLOTS, detect, 0)

    def spread(step, ring):
        return [remote(smis.at[step], misr.at[step, k], s_m.at[step, k], r_m.at[step, k], ring[k]) for k in range(7)]

    spreads = [spread(i, ring) for i, ring in enumerate((ring_z, ring_y, ring_x))]

    def send_mis(step):
        smis[step] = mis[...]
        for q in spreads[step]:
            q.start()

    def take_mis(step):
        total = mis[...]
        for k, q in enumerate(spreads[step]):
            q.wait_recv()
            total = total + misr[step, k]
        mis[...] = total

    send_mis(0)

    give_x = [remote(gc.at[s, give], xbuf.at[s], s_x.at[s], r_x.at[s], sibling) for s in range(SLICES)]
    send_r = [remote(sbuf.at[s], rbuf.at[s, keep], s_r.at[s], r_r.at[s, keep], dev(x, yl, oh, z, h)) for s in range(SLICES)]
    got_r = [[remote(sbuf.at[s], rbuf.at[s, ch], s_r.at[s], r_r.at[s, ch], sibling) for ch in range(2)] for s in range(SLICES)]
    send_rn = [remote(gn.at[s], rbuf.at[s], s_rn.at[s], r_rn.at[s], dev(x, yl, h, lax.rem(z + ZS - dz, ZS), h)) for s in range(SLICES)]

    def patch_grad(s):
        gn[s] = jnp.zeros((2, ROWS, N), F32)
        gc[s] = jnp.zeros((2, ROWS, N), F32)

        def one(p, carry):
            t = trans_at(s, p)
            parts = [cmulc(psi_at(s, p, m), pair(wav, p, m)) for m in range(MODES)]
            tg = (parts[0][0] + parts[1][0] + parts[2][0] + parts[3][0], parts[0][1] + parts[1][1] + parts[2][1] + parts[3][1])
            q = cmulc(t, tg)
            in_n, in_c, col = masks(p, ROWS)
            row = meta[0, p]
            for ch, value in enumerate((q[1], -q[0])):
                gp[ch, 64 : 64 + N, :] = pltpu.roll(value, col, 1)
                placed = gp[ch, pl.ds(64 - row, ROWS), :]
                gn[s, ch] = gn[s, ch] + jnp.where(in_n, placed, 0.0)
                gc[s, ch] = gc[s, ch] + jnp.where(in_c, placed, 0.0)
            return carry

        lax.fori_loop(0, SLOTS, one, 0)
        give_x[s].start()

        @pl.when(guest)
        def _():
            send_rn[s].start()

    def back(s):
        def one(p, carry):
            t = trans_at(s, p)
            kern = pair(kern_in)
            waves = dft([cmulc(t, pair(wav, p, m)) for m in range(MODES)], fwd_in[...], inv_in[...])
            waves = dft([cmulc(kern, w) for w in waves], inv_in[...], fwd_in[...])
            for m in range(MODES):
                put(wav, waves[m], p, m)
            return carry

        lax.fori_loop(0, SLOTS, one, 0)

    def hand_over(s):
        give_x[s].wait_recv()
        sbuf[s] = gc[s, keep] + xbuf[s]
        send_r[s].start()

    for s in reversed(range(1, SLICES)):
        patch_grad(s)
        back(s)
        hand_over(s)
        if s == 3:
            take_mis(0)
            send_mis(1)
        if s == 2:
            take_mis(1)
            send_mis(2)
    patch_grad(0)

    pacc[...] = jnp.zeros_like(pacc)

    def probe_slot(p, carry):
        t = trans_at(0, p)
        for m in range(MODES):
            w = cmulc(t, pair(wav, p, m))
            put(pacc, (pacc[m, :, 0:N] + w[0], pacc[m, :, N : 2 * N] + w[1]), m)
        return carry

    lax.fori_loop(0, SLOTS, probe_slot, 0)
    for zz in range(ZS):
        for hh in range(2):
            at = (2 * zz + hh) * 8
            for m in range(MODES):
                pgr[hh, zz, m] = pacc[m, at : at + 8, :]
    give_p = remote(pgr.at[oc], px, s_px, r_px, sibling)
    give_p.start()
    hand_over(0)
    give_p.wait_recv()
    px[...] = px[...] + pgr[c]
    send_q = [remote(px.at[at_z(k)], pzr.at[k - 1], s_pq.at[k - 1], r_pq.at[k - 1], ring_z[k - 1]) for k in range(1, ZS)]
    for k in (3, 2, 4, 1, 5, 0, 6):
        send_q[k].start()
    take_mis(2)
    total = mis[...]
    misfit = jnp.sum(jnp.sum(total[0:8], axis=0, keepdims=True), axis=1, keepdims=True)
    slots = total[8:9, 0:1]
    scale = 1.0 / jnp.sqrt(misfit / (slots * N * N) + 1e-06)
    for q in send_q:
        q.wait_recv()
    done = px[z]
    for k in range(ZS - 1):
        done = done + pzr[k]
    pfin[...] = done
    send_po = remote(pfin, pown, s_po, r_po, dev(x, yl, oh, z, h))

    @pl.when(guest)
    def _():
        send_po.start()

    @pl.when(nat)
    def _():
        out_probe[0] = pfin[...] * scale
        for s in reversed(range(SLICES)):
            send_rn[s].wait_recv()
            out_obj[s] = (gn[s] + rbuf[s]) * scale

    @pl.when(guest)
    def _():
        for s in reversed(range(SLICES)):
            for ch in range(2):
                got_r[s][ch].wait_recv()
            out_obj[s] = rbuf[s] * scale
        send_po.wait_recv()
        out_probe[0] = pown[...] * scale

    @pl.when(guest)
    def _():
        to_probe.wait_send()
        to_meta.wait_send()
        to_amp.wait_send()
        for s in range(SLICES):
            for ch in range(2):
                to_c[s][ch].wait_send()
            send_rn[s].wait_send()
        send_po.wait_send()

    @pl.when(nat)
    def _():
        for s in range(SLICES):
            to_n[s].wait_send()

    @pl.when(along)
    def _():
        to_metan.wait_send()
        to_ampn.wait_send()

    for k in range(ZS - 1):
        own_probe[k].wait_send()
        send_q[k].wait_send()
        for step in range(3):
            spreads[step][k].wait_send()
    fwd_p.wait_send()
    give_p.wait_send()
    for s in range(SLICES):
        fwd_c[s].wait_send()
        give_x[s].wait_send()
        send_r[s].wait_send()


def body(potential, probe, amplitudes, row_offset, col_offset, counts):
    forward, inverse = tables()
    kern = propagator()
    vmem = pl.BlockSpec(memory_space=pltpu.VMEM)
    smem = pl.BlockSpec(memory_space=pltpu.SMEM)
    hbm = pl.BlockSpec(memory_space=pl.ANY)
    dma = pltpu.SemaphoreType.DMA
    tile = (SLICES, 2, ROWS, N)
    wave = (MODES, N, 2 * N)
    chunk = (MODES, 8, 2 * N)

    def f32(*shape):
        return pltpu.VMEM(shape, F32)

    return pl.pallas_call(
        kernel,
        out_shape=(jax.ShapeDtypeStruct(tile, F32), jax.ShapeDtypeStruct((1, *chunk), F32)),
        in_specs=[hbm, hbm, vmem, smem, smem, smem, vmem, vmem, vmem],
        out_specs=(vmem, vmem),
        scratch_shapes=[
            *[f32(*tile[1:])] * 8, f32(*tile), f32(*tile), f32(*tile),
            f32(SLICES, ROWS, N), f32(SLICES, ROWS, N),
            f32(SLOTS, N, N), f32(SLOTS, N, N),
            pltpu.VMEM((8, N), jnp.int32), pltpu.VMEM((8, N), jnp.int32), pltpu.SMEM((8, N), jnp.int32),
            f32(2, ZS, *chunk), f32(*wave), f32(SLICES - 1, SLOTS, *wave), f32(SLOTS, *wave),
            f32(SLICES, SLOTS, 2, N, N), f32(2, 256, N),
            f32(*wave), f32(2, ZS, *chunk), f32(ZS, *chunk), f32(ZS - 1, *chunk), f32(*chunk), f32(*chunk),
            f32(16, N), f32(3, 7, 16, N), f32(3, 16, N),
            dma((8,)), dma((3,)), dma, dma, dma,
            dma((4,)), dma((4,)), dma((4, 2)), dma((4,)), dma((4,)), dma((4,)),
            dma((7,)), dma((7,)), dma, dma,
            dma((4,)), dma((4,)), dma((4,)), dma((4, 2)), dma((4,)), dma((4,)),
            dma, dma, dma((7,)), dma((7,)), dma, dma, dma((3, 7)), dma((3, 7)),
        ],
        compiler_params=pltpu.CompilerParams(collective_id=0, has_side_effects=True),
        name="ptycho",
    )(potential, probe, amplitudes, row_offset, col_offset, counts, forward, inverse, kern)


def solution(mesh):
    placed = (
        P(None, None, "group", "pos"),
        P("group", None, "pos", None),
        P("group", "pos", None, None, None),
        P("group", "pos", None),
        P("group", "pos", None),
        P("group", "pos"),
    )
    return jax.shard_map(
        body,
        mesh=mesh,
        in_specs=placed,
        out_specs=(P(None, None, "group", "pos"), P("group", None, "pos", None)),
        check_vma=False,
    )
```

time: 468 us -> 87.1 us (0.19)
  the two profiles are of different devices: /device:TPU:2 before, /device:TPU:1 now
where the time goes in v1:
time: 87.1 us; the launch traced here: 86.9 us
  Pallas kernels  83 us (95%)
  local copies, waits for them, and re-layouts  2.69 us (3%)
  between operations  1.29 us (1%)
    pallas_call x1, Pallas kernels, body(): pl.pallas_call(kernel, out_shape=(jax.ShapeDtypeStruct(tile, F32), jax.Sh...  83 us
    unnamed x4, local copies, waits for them, and re-layouts  2.69 us

profile of v1, /device:TPU:1, one launch (start us, length us, event | category | flops | bytes accessed | tf_op | source)
XLA Modules:
  0.0 86.9 jit_solution(1133471861400373670)
XLA Ops:
  1.3 83.0 %ptycho.1 = (f32[4,2,192,128]{3,2,1,0:T(8,128)}, f32[1,4,8,256]{3,2,1,0:T(8,128)}) custom-call(f32[4,2,192,128]{3,2,1,0:T(8,128)} %pot.1, f32[1,4,8,256]{3,2,1,0:T(8,128)} %probe.1, bf16[1,1,3,128,128]{4,3,2,1,0:T(8,128)(2,1)} %amps_in.1, s32[1,1,3]{2,1,0:T(1,128)} %row_in.1, s32[1,1,3]{2,1,0:T(1,128)} %col_in.1, s32[1,1]{1,0:T(1,128)S(6)} %copy.13.cnt_in, ...), custom_call_target="tpu_custom_call" | custom-call | tf_op jit(solution)/shard_map/ptycho/pallas_call | solution.py:519
  84.2 0.0 copy-start
  84.3 2.1 %copy.14 = f32[4,2,192,128]{3,2,1,0:T(8,128)} copy(f32[4,2,192,128]{3,2,1,0:T(8,128)} %get-tuple-element.4) | data formatting | bytes 1572864
  86.3 0.0 copy-done
  86.3 0.6 copy.15
Async XLA Ops:
  84.2 2.1 %copy-start = (f32[1,4,8,256]{3,2,1,0:T(8,128)S(1)}, f32[1,4,8,256]{3,2,1,0:T(8,128)}, u32[]{:S(2)}) copy-start(f32[1,4,8,256]{3,2,1,0:T(8,128)} %get-tuple-element.5) | copy-start | bytes 98308

commit v2 on v1

--- a/solution.py
+++ b/solution.py
@@ -61,11 +61,11 @@
 
 
 def kernel(
-    pot, probe, amps_in, row_in, col_in, cnt_in, fwd_in, inv_in, kern_in,
-    out_obj, out_probe,
+    pot, probe, amps_in, row_in, col_in, cnt_in, fwd_hbm, inv_hbm, kern_hbm,
+    out_obj, out_probe, out_scale,
     n0, n1, n2, n3, c0, c1, c2, c3, gn, gc, rbuf, xbuf, sbuf, amps, amps_out, metav, meta_out, meta,
-    pbuf, psi0, psi, wav, tr, gp, pacc, pgr, px, pzr, pown, pfin,
-    mis, misr, smis,
+    pbuf, psi, wav, tr, gp, pgr, px, pzr, pown, pfin,
+    mis, misr, smis, stage, chunk, stage_sem, amps_raw, fwd_in, inv_in, kern_in,
     loc_sem, s_misc, r_probe, r_meta, r_amp,
     s_n, r_n, s_c, r_c, s_f, r_f, s_pz, r_pz, s_pf, r_pf,
     s_x, r_x, s_r, r_r, s_rn, r_rn, s_px, r_px, s_pq, r_pq, s_po, r_po, s_m, r_m,
@@ -110,6 +110,12 @@
     for partner in partners:
         pl.semaphore_signal(barrier, inc=1, device_id=partner)
 
+    own_pot = [pltpu.make_async_copy(pot.at[s], stage.at[s], stage_sem.at[s]) for s in range(SLICES)]
+    own_p = pltpu.make_async_copy(probe.at[0], chunk, stage_sem.at[4])
+    own_p.start()
+    for s in range(SLICES):
+        own_pot[s].start()
+
     lane = lax.broadcasted_iota(jnp.int32, (8, N), 1)
     packed = jnp.zeros((8, N), jnp.int32)
     for p in range(SLOTS):
@@ -117,26 +123,34 @@
         packed = jnp.where(lane == SLOTS + p, col_in[0, 0, p], packed)
     packed = jnp.where(lane == 2 * SLOTS, cnt_in[0, 0], packed)
     meta_out[...] = packed
-    for p in range(SLOTS):
-        amps_out[p] = amps_in[0, 0, p].astype(F32)
-    gp[...] = jnp.zeros_like(gp)
+    own_a = pltpu.make_async_copy(amps_in.at[0, 0], amps_raw, stage_sem.at[5])
+    consts = [pltpu.make_async_copy(src, dst, stage_sem.at[6 + i]) for i, (src, dst) in enumerate(((fwd_hbm, fwd_in), (inv_hbm, inv_in), (kern_hbm, kern_in)))]
+    own_a.start()
+    for q in consts:
+        q.start()
 
     pl.semaphore_wait(barrier, len(partners))
 
-    to_probe = remote(probe.at[0], pbuf.at[h, z], s_misc.at[0], r_probe, dev(x, yl, oh, z, oc))
+    def half_of(ref, hh):
+        return ref.at[:, :, pl.ds(pl.multiple_of(hh * 8, 8), 8), :]
+
+    def chunk_of(ref, zz, hh):
+        return ref.at[:, zz, pl.ds(pl.multiple_of(hh * 8, 8), 8), :]
+
+    to_probe = remote(chunk, chunk_of(pbuf, z, h), s_misc.at[0], r_probe, dev(x, yl, oh, z, oc))
     to_meta = remote(meta_out, metav, s_misc.at[1], r_meta, dev(x, yl, oh, z, 1))
     to_amp = remote(amps_out, amps, s_misc.at[2], r_amp, dev(x, yl, oh, z, 1))
     to_metan = remote(meta_out, metav, s_misc.at[1], r_meta, dev(x, yl, h, at_z(1), 0))
     to_ampn = remote(amps_out, amps, s_misc.at[2], r_amp, dev(x, yl, h, at_z(1), 0))
-    to_n = [remote(pot.at[s], nbuf[s], s_n.at[s], r_n.at[s], dev(x, yl, h, lax.rem(z + dz, ZS), oc)) for s in range(SLICES)]
+    to_n = [remote(stage.at[s], nbuf[s], s_n.at[s], r_n.at[s], dev(x, yl, h, lax.rem(z + dz, ZS), oc)) for s in range(SLICES)]
     to_c = [
-        [remote(pot.at[s, ch], cbuf[s].at[ch], s_c.at[s, ch], r_c.at[s], dev(x, yl, oh, z, c if ch == 0 else oc)) for ch in range(2)]
+        [remote(stage.at[s, ch], cbuf[s].at[ch], s_c.at[s, ch], r_c.at[s], dev(x, yl, oh, z, c if ch == 0 else oc)) for ch in range(2)]
         for s in range(SLICES)
     ]
-    own_probe = [remote(probe.at[0], pbuf.at[c, z], s_pz.at[k], r_pz.at[k], ring_z[k]) for k in range(ZS - 1)]
-    got_probe = [remote(pbuf.at[c, z], pbuf.at[c, z], s_pz.at[k], r_pz.at[k], ring_z[k]) for k in range(ZS - 1)]
-    loc_n = [pltpu.make_async_copy(pot.at[s], nbuf[s], loc_sem.at[s]) for s in range(SLICES)]
-    loc_p = pltpu.make_async_copy(probe.at[0], pbuf.at[c, z], loc_sem.at[4])
+    own_probe = [remote(chunk, chunk_of(pbuf, z, c), s_pz.at[k], r_pz.at[k], ring_z[k]) for k in range(ZS - 1)]
+    got_probe = [remote(chunk_of(pbuf, z, c), chunk_of(pbuf, z, c), s_pz.at[k], r_pz.at[k], ring_z[k]) for k in range(ZS - 1)]
+    loc_n = [pltpu.make_async_copy(stage.at[s], nbuf[s], loc_sem.at[s]) for s in range(SLICES)]
+    loc_p = pltpu.make_async_copy(chunk, chunk_of(pbuf, z, c), loc_sem.at[4])
     loc_a = pltpu.make_async_copy(amps_out, amps, loc_sem.at[5])
     loc_m = pltpu.make_async_copy(meta_out, metav, loc_sem.at[6])
     loc_s = pltpu.make_async_copy(metav, meta, loc_sem.at[7])
@@ -145,38 +159,64 @@
 
     @pl.when(guest)
     def _():
+        to_meta.start()
+
+    @pl.when(along)
+    def _():
+        to_metan.start()
+
+    @pl.when(here)
+    def _():
+        loc_m.start()
+
+    own_p.wait()
+
+    @pl.when(guest)
+    def _():
         to_probe.start()
-        to_meta.start()
-        for s in range(SLICES):
-            for ch in range(2):
-                to_c[s][ch].start()
-        to_amp.start()
+
+    own_pot[0].wait()
+
+    @pl.when(guest)
+    def _():
+        for ch in range(2):
+            to_c[0][ch].start()
 
     @pl.when(nat)
     def _():
+        to_n[0].start()
         for k in (0, 6, 1, 5, 2, 4, 3):
             own_probe[k].start()
         loc_p.start()
-        for s in range(SLICES):
+        loc_n[0].start()
+
+    for s in range(1, SLICES):
+        own_pot[s].wait()
+
+        @pl.when(guest)
+        def _(s=s):
+            for ch in range(2):
+                to_c[s][ch].start()
+
+        @pl.when(nat)
+        def _(s=s):
             loc_n[s].start()
 
-    @pl.when(along)
-    def _():
-        to_metan.start()
+    own_a.wait()
+    for p in range(SLOTS):
+        amps_out[p] = amps_raw[p].astype(F32)
+
+    @pl.when(guest)
+    def _():
+        to_amp.start()
 
     @pl.when(here)
     def _():
         loc_a.start()
-        loc_m.start()
-
-    @pl.when(nat)
-    def _():
-        for s in range(SLICES):
-            to_n[s].start()
-
-    @pl.when(along)
-    def _():
-        to_ampn.start()
+
+    gp[...] = jnp.zeros_like(gp)
+    for q in consts:
+        q.wait()
 
     @pl.when(here)
     def _():
@@ -260,7 +300,10 @@
         ref[(*at, slice(None), slice(N, 2 * N))] = value[1]
 
     def psi_at(s, p, m):
-        return pair(psi0, m) if s == 0 else pair(psi, s - 1, p, m)
+        if s:
+            return pair(psi, s - 1, p, m)
+        whole = pbuf[m].reshape(N, 2 * N)
+        return whole[:, 0:N], whole[:, N : 2 * N]
 
     def trans_at(s, p):
         return tr[s, p, 0], tr[s, p, 1]
@@ -278,18 +321,28 @@
         lax.fori_loop(0, SLOTS, one, 0)
 
     pass_on(0)
+
+    @pl.when(nat)
+    def _():
+        to_n[1].start()
+
     transmit(0)
     for k in range(ZS - 1):
         own_probe[k].wait_recv()
-    fwd_p = remote(pbuf.at[c], pbuf.at[c], s_pf, r_pf, sibling)
+    fwd_p = remote(half_of(pbuf, c), half_of(pbuf, c), s_pf, r_pf, sibling)
     fwd_p.start()
     pass_on(1)
     fwd_p.wait_recv()
-    for zz in range(ZS):
-        for hh in range(2):
-            at = (2 * zz + hh) * 8
-            for m in range(MODES):
-                psi0[m, at : at + 8, :] = pbuf[hh, zz, m]
+
+    @pl.when(nat)
+    def _():
+        for s in range(2, SLICES):
+            to_n[s].start()
+
+    @pl.when(along)
+    def _():
+        to_ampn.start()
+
     prop(0)
     pass_on(2)
     transmit(1)
@@ -299,22 +352,30 @@
     prop(2)
     transmit(3)
 
-    @pl.when(here)
-    def _():
-        loc_a.wait()
-
-    @pl.when(jnp.logical_not(here))
-    def _():
-        to_amp.wait_recv()
-
     count = meta[0, 2 * SLOTS]
     mis[0:8, :] = jnp.zeros((8, N), F32)
     mis[8:16, :] = jnp.zeros((8, N), F32) + count.astype(F32)
 
+    def spectrum(p, carry):
+        t = trans_at(SLICES - 1, p)
+        far = dft([cmul(t, psi_at(SLICES - 1, p, m)) for m in range(MODES)], fwd_in[...], inv_in[...])
+        for m in range(MODES):
+            put(wav, far[m], p, m)
+        return carry
+
+    lax.fori_loop(0, SLOTS, spectrum, 0)
+
+    @pl.when(here)
+    def _():
+        loc_a.wait()
+
+    @pl.when(jnp.logical_not(here))
+    def _():
+        to_amp.wait_recv()
+
     def detect(p, carry):
         weight = jnp.where(p < count, 1.0, 0.0)
-        t = trans_at(SLICES - 1, p)
-        far = dft([cmul(t, psi_at(SLICES - 1, p, m)) for m in range(MODES)], fwd_in[...], inv_in[...])
+        far = [pair(wav, p, m) for m in range(MODES)]
         inten = far[0][0] * far[0][0] + far[0][1] * far[0][1]
         for m in range(1, MODES):
             inten = inten + (far[m][0] * far[m][0] + far[m][1] * far[m][1])
@@ -337,7 +398,7 @@
     def spread(step, ring):
         return [remote(smis.at[step], misr.at[step, k], s_m.at[step, k], r_m.at[step, k], ring[k]) for k in range(7)]
 
-    spreads = [spread(i, ring) for i, ring in enumerate((ring_z, ring_y, ring_x))]
+    spreads = [spread(i, ring) for i, ring in enumerate((ring_z, ring_x, ring_y))]
 
     def send_mis(step):
         smis[step] = mis[...]
@@ -379,7 +440,7 @@
         lax.fori_loop(0, SLOTS, one, 0)
         give_x[s].start()
 
-        @pl.when(guest)
+        @pl.when(jnp.logical_and(guest, s > 0))
         def _():
             send_rn[s].start()
 
@@ -404,69 +465,73 @@
         patch_grad(s)
         back(s)
         hand_over(s)
-        if s == 3:
+        if s == 2:
             take_mis(0)
             send_mis(1)
-        if s == 2:
-            take_mis(1)
-            send_mis(2)
-    patch_grad(0)
-
-    pacc[...] = jnp.zeros_like(pacc)
+
+    pgr[...] = jnp.zeros_like(pgr)
 
     def probe_slot(p, carry):
         t = trans_at(0, p)
         for m in range(MODES):
-            w = cmulc(t, pair(wav, p, m))
-            put(pacc, (pacc[m, :, 0:N] + w[0], pacc[m, :, N : 2 * N] + w[1]), m)
+            w = jnp.concatenate(cmulc(t, pair(wav, p, m)), 1)
+            pgr[m] = pgr[m] + w.reshape(ZS, 16, 2 * N)
         return carry
 
     lax.fori_loop(0, SLOTS, probe_slot, 0)
-    for zz in range(ZS):
-        for hh in range(2):
-            at = (2 * zz + hh) * 8
-            for m in range(MODES):
-                pgr[hh, zz, m] = pacc[m, at : at + 8, :]
-    give_p = remote(pgr.at[oc], px, s_px, r_px, sibling)
+    give_p = remote(half_of(pgr, oc), px, s_px, r_px, sibling)
     give_p.start()
-    hand_over(0)
+    patch_grad(0)
     give_p.wait_recv()
-    px[...] = px[...] + pgr[c]
-    send_q = [remote(px.at[at_z(k)], pzr.at[k - 1], s_pq.at[k - 1], r_pq.at[k - 1], ring_z[k - 1]) for k in range(1, ZS)]
+    px[...] = px[...] + pgr[:, :, pl.ds(pl.multiple_of(c * 8, 8), 8), :]
+    send_q = [remote(px.at[:, at_z(k)], pzr.at[k - 1], s_pq.at[k - 1], r_pq.at[k - 1], ring_z[k - 1]) for k in range(1, ZS)]
     for k in (3, 2, 4, 1, 5, 0, 6):
         send_q[k].start()
+
+    @pl.when(guest)
+    def _():
+        send_rn[0].start()
+
+    hand_over(0)
+    take_mis(1)
+    send_mis(2)
+    for q in send_q:
+        q.wait_recv()
+    done = px[:, z]
+    for k in range(ZS - 1):
+        done = done + pzr[k]
+    send_po = remote(pfin, pown, s_po, r_po, dev(x, yl, oh, z, h))
+
+    @pl.when(guest)
+    def _():
+        pfin[...] = done
+        send_po.start()
+
+    out_n = [pltpu.make_async_copy(gn.at[s], out_obj.at[s], loc_sem.at[s]) for s in range(SLICES)]
+    out_r = [pltpu.make_async_copy(rbuf.at[s], out_obj.at[s], loc_sem.at[s]) for s in range(SLICES)]
+
+    @pl.when(nat)
+    def _():
+        out_probe[0] = done
+        for s in reversed(range(SLICES)):
+            send_rn[s].wait_recv()
+            gn[s] = gn[s] + rbuf[s]
+            out_n[s].start()
+
+    @pl.when(guest)
+    def _():
+        for s in reversed(range(SLICES)):
+            for ch in range(2):
+                got_r[s][ch].wait_recv()
+            out_r[s].start()
+        send_po.wait_recv()
+        out_probe[0] = pown[...]
+
     take_mis(2)
     total = mis[...]
     misfit = jnp.sum(jnp.sum(total[0:8], axis=0, keepdims=True), axis=1, keepdims=True)
     slots = total[8:9, 0:1]
-    scale = 1.0 / jnp.sqrt(misfit / (slots * N * N) + 1e-06)
-    for q in send_q:
-        q.wait_recv()
-    done = px[z]
-    for k in range(ZS - 1):
-        done = done + pzr[k]
-    pfin[...] = done
-    send_po = remote(pfin, pown, s_po, r_po, dev(x, yl, oh, z, h))
-
-    @pl.when(guest)
-    def _():
-        send_po.start()
-
-    @pl.when(nat)
-    def _():
-        out_probe[0] = pfin[...] * scale
-        for s in reversed(range(SLICES)):
-            send_rn[s].wait_recv()
-            out_obj[s] = (gn[s] + rbuf[s]) * scale
-
-    @pl.when(guest)
-    def _():
-        for s in reversed(range(SLICES)):
-            for ch in range(2):
-                got_r[s][ch].wait_recv()
-            out_obj[s] = rbuf[s] * scale
-        send_po.wait_recv()
-        out_probe[0] = pown[...] * scale
+    out_scale[...] = jnp.broadcast_to(1.0 / jnp.sqrt(misfit / (slots * N * N) + 1e-06), (8, N))
 
     @pl.when(guest)
     def _():
@@ -497,9 +562,31 @@
     fwd_p.wait_send()
     give_p.wait_send()
     for s in range(SLICES):
+        out_n[s].wait()
         fwd_c[s].wait_send()
         give_x[s].wait_send()
         send_r[s].wait_send()
+
+
+def finish(obj, pgrad, scale, out_obj, out_probe, held, held_probe, factor, in_sem, out_sem):
+    loads = [pltpu.make_async_copy(scale, factor, in_sem.at[SLICES])]
+    loads += [pltpu.make_async_copy(obj.at[s], held.at[s], in_sem.at[s]) for s in range(SLICES)]
+    loads.append(pltpu.make_async_copy(pgrad, held_probe, in_sem.at[SLICES + 1]))
+    stores = [pltpu.make_async_copy(held.at[s], out_obj.at[s], out_sem.at[s]) for s in range(SLICES)]
+    stores.append(pltpu.make_async_copy(held_probe, out_probe, out_sem.at[SLICES]))
+    for load in loads:
+        load.start()
+    loads[0].wait()
+    by = factor[0:1, 0:1]
+    for s in range(SLICES):
+        loads[s + 1].wait()
+        held[s] = held[s] * by
+        stores[s].start()
+    loads[-1].wait()
+    held_probe[...] = held_probe[...] * by
+    stores[-1].start()
+    for store in stores:
+        store.wait()
 
 
 def body(potential, probe, amplitudes, row_offset, col_offset, counts):
@@ -507,7 +594,7 @@
     kern = propagator()
     vmem = pl.BlockSpec(memory_space=pltpu.VMEM)
     smem = pl.BlockSpec(memory_space=pltpu.SMEM)
-    hbm = pl.BlockSpec(memory_space=pl.ANY)
+    hbm = pl.BlockSpec(memory_space=pltpu.HBM)
     dma = pltpu.SemaphoreType.DMA
     tile = (SLICES, 2, ROWS, N)
     wave = (MODES, N, 2 * N)
@@ -516,20 +603,21 @@
     def f32(*shape):
         return pltpu.VMEM(shape, F32)
 
-    return pl.pallas_call(
+    obj, pgrad, scale = pl.pallas_call(
         kernel,
-        out_shape=(jax.ShapeDtypeStruct(tile, F32), jax.ShapeDtypeStruct((1, *chunk), F32)),
-        in_specs=[hbm, hbm, vmem, smem, smem, smem, vmem, vmem, vmem],
-        out_specs=(vmem, vmem),
+        out_shape=tuple(jax.ShapeDtypeStruct(shape, F32) for shape in (tile, (1, *chunk), (8, N))),
+        in_specs=[hbm, hbm, hbm, smem, smem, smem, hbm, hbm, hbm],
+        out_specs=(hbm, vmem, vmem),
         scratch_shapes=[
             *[f32(*tile[1:])] * 8, f32(*tile), f32(*tile), f32(*tile),
             f32(SLICES, ROWS, N), f32(SLICES, ROWS, N),
             f32(SLOTS, N, N), f32(SLOTS, N, N),
             pltpu.VMEM((8, N), jnp.int32), pltpu.VMEM((8, N), jnp.int32), pltpu.SMEM((8, N), jnp.int32),
-            f32(2, ZS, *chunk), f32(*wave), f32(SLICES - 1, SLOTS, *wave), f32(SLOTS, *wave),
+            f32(MODES, ZS, 16, 2 * N), f32(SLICES - 1, SLOTS, *wave), f32(SLOTS, *wave),
             f32(SLICES, SLOTS, 2, N, N), f32(2, 256, N),
-            f32(*wave), f32(2, ZS, *chunk), f32(ZS, *chunk), f32(ZS - 1, *chunk), f32(*chunk), f32(*chunk),
-            f32(16, N), f32(3, 7, 16, N), f32(3, 16, N),
+            f32(MODES, ZS, 16, 2 * N), f32(MODES, ZS, 8, 2 * N), f32(ZS - 1, *chunk), f32(*chunk), f32(*chunk),
+            f32(16, N), f32(3, 7, 16, N), f32(3, 16, N), f32(*tile), f32(*chunk), dma((9,)),
+            pltpu.VMEM((SLOTS, N, N), BF16), pltpu.VMEM((2 * N, 2 * N), BF16), pltpu.VMEM((2 * N, 2 * N), BF16), f32(N, 2 * N),
             dma((8,)), dma((3,)), dma, dma, dma,
             dma((4,)), dma((4,)), dma((4, 2)), dma((4,)), dma((4,)), dma((4,)),
             dma((7,)), dma((7,)), dma, dma,
@@ -539,6 +627,14 @@
         compiler_params=pltpu.CompilerParams(collective_id=0, has_side_effects=True),
         name="ptycho",
     )(potential, probe, amplitudes, row_offset, col_offset, counts, forward, inverse, kern)
+    return pl.pallas_call(
+        finish,
+        out_shape=tuple(jax.ShapeDtypeStruct(shape, F32) for shape in (tile, (1, *chunk))),
+        in_specs=[hbm, hbm, hbm],
+        out_specs=(hbm, hbm),
+        scratch_shapes=[f32(*tile), f32(1, *chunk), f32(8, N), dma((SLICES + 2,)), dma((SLICES + 1,))],
+        name="scale",
+    )(obj, pgrad, scale)
 
 
 def solution(mesh):

time: 87.1 us -> 78.3 us (0.90); the launches traced: 86.9 us -> 77.2 us
  Pallas kernels: 83 us -> 75.9 us
  local copies, waits for them, and re-layouts: 2.69 us -> 0 us
    pallas_call x1 -> x2, Pallas kernels: 83 us -> 75.9 us  [the longest x1 73.9 us: body(): pl.pallas_call(kernel, out_shape=tuple((jax.ShapeDtypeStruct(shape, F32)...]
    unnamed x4 -> x0, local copies, waits for them, and re-layouts: 2.69 us -> none
where the time goes in v2:
time: 78.3 us; the launch traced here: 77.2 us
  Pallas kernels  75.9 us (97%)
  between operations  1.29 us (2%)
    pallas_call x1, Pallas kernels, body(): pl.pallas_call(kernel, out_shape=tuple((jax.ShapeDtypeStruct(shape, F32)...  73.9 us
    pallas_call x1, Pallas kernels, body(): pl.pallas_call(finish, out_shape=tuple((jax.ShapeDtypeStruct(shape, F32)...  2.01 us

profile of v2, /device:TPU:1, one launch (start us, length us, event | category | flops | bytes accessed | tf_op | source)
XLA Modules:
  0.0 77.2 jit_solution(11452721468059797844)
XLA Ops:
  1.3 73.9 %ptycho.1 = (f32[4,2,192,128]{3,2,1,0:T(8,128)}, f32[1,4,8,256]{3,2,1,0:T(8,128)}, f32[8,128]{1,0:T(8,128)}) custom-call(f32[4,2,192,128]{3,2,1,0:T(8,128)} %pot.1, f32[1,4,8,256]{3,2,1,0:T(8,128)} %probe.1, bf16[1,1,3,128,128]{4,3,2,1,0:T(8,128)(2,1)} %amps_in.1, s32[1,1,3]{2,1,0:T(1,128)} %row_in.1, s32[1,1,3]{2,1,0:T(1,128)} %col_in.1, ...), custom_call_target="tpu_custom_call" | custom-call | tf_op jit(solution)/shard_map/ptycho/pallas_call | solution.py:606
  75.2 2.0 %scale.1 = (f32[4,2,192,128]{3,2,1,0:T(8,128)}, f32[1,4,8,256]{3,2,1,0:T(8,128)}) custom-call(f32[4,2,192,128]{3,2,1,0:T(8,128)} %get-tuple-element.5.obj, f32[1,4,8,256]{3,2,1,0:T(8,128)} %get-tuple-element.6.pgrad, f32[8,128]{1,0:T(8,128)} %get-tuple-element.7.scale), custom_call_target="tpu_custom_call" | custom-call | tf_op jit(solution)/shard_map/scale/pallas_call | solution.py:630

commit v3 on v2

--- a/solution.py
+++ b/solution.py
@@ -290,7 +290,7 @@
             tr[s, p, 1] = mag * jnp.sin(parts[0])
             return carry
 
-        lax.fori_loop(0, SLOTS, one, 0)
+        lax.fori_loop(0, SLOTS, one, 0, unroll=True)
 
     def pair(ref, *at):
         return ref[(*at, slice(None), slice(0, N))], ref[(*at, slice(None), slice(N, 2 * N))]
@@ -318,7 +318,7 @@
                 put(psi, waves[m], s, p, m)
             return carry
 
-        lax.fori_loop(0, SLOTS, one, 0)
+        lax.fori_loop(0, SLOTS, one, 0, unroll=True)
 
     pass_on(0)
 
@@ -363,7 +363,7 @@
             put(wav, far[m], p, m)
         return carry
 
-    lax.fori_loop(0, SLOTS, spectrum, 0)
+    lax.fori_loop(0, SLOTS, spectrum, 0, unroll=True)
 
     @pl.when(here)
     def _():
@@ -393,7 +393,7 @@
             put(wav, waves[m], p, m)
         return carry
 
-    lax.fori_loop(0, SLOTS, detect, 0)
+    lax.fori_loop(0, SLOTS, detect, 0, unroll=True)
 
     def spread(step, ring):
         return [remote(smis.at[step], misr.at[step, k], s_m.at[step, k], r_m.at[step, k], ring[k]) for k in range(7)]
@@ -437,7 +437,7 @@
                 gc[s, ch] = gc[s, ch] + jnp.where(in_c, placed, 0.0)
             return carry
 
-        lax.fori_loop(0, SLOTS, one, 0)
+        lax.fori_loop(0, SLOTS, one, 0, unroll=True)
         give_x[s].start()
 
         @pl.when(jnp.logical_and(guest, s > 0))
@@ -454,7 +454,7 @@
                 put(wav, waves[m], p, m)
             return carry
 
-        lax.fori_loop(0, SLOTS, one, 0)
+        lax.fori_loop(0, SLOTS, one, 0, unroll=True)
 
     def hand_over(s):
         give_x[s].wait_recv()

time: 78.3 us -> 73.6 us (0.940); the launches traced: 77.2 us -> 73.4 us
  Pallas kernels: 75.9 us -> 72 us
    pallas_call x1, Pallas kernels: 73.9 us -> 70 us  [body(): pl.pallas_call(kernel, out_shape=tuple((jax.ShapeDtypeStruct(shape, F32)...]
where the time goes in v3:
time: 73.6 us; the launch traced here: 73.4 us
  Pallas kernels  72 us (98%)
  between operations  1.45 us (2%)
    pallas_call x1, Pallas kernels, body(): pl.pallas_call(kernel, out_shape=tuple((jax.ShapeDtypeStruct(shape, F32)...  70 us
    pallas_call x1, Pallas kernels, body(): pl.pallas_call(finish, out_shape=tuple((jax.ShapeDtypeStruct(shape, F32)...  2.01 us

profile of v3, /device:TPU:1, one launch (start us, length us, event | category | flops | bytes accessed | tf_op | source)
XLA Modules:
  0.0 73.4 jit_solution(5586108578998106318)
XLA Ops:
  1.3 70.0 %ptycho.1 = (f32[4,2,192,128]{3,2,1,0:T(8,128)}, f32[1,4,8,256]{3,2,1,0:T(8,128)}, f32[8,128]{1,0:T(8,128)}) custom-call(f32[4,2,192,128]{3,2,1,0:T(8,128)} %pot.1, f32[1,4,8,256]{3,2,1,0:T(8,128)} %probe.1, bf16[1,1,3,128,128]{4,3,2,1,0:T(8,128)(2,1)} %amps_in.1, s32[1,1,3]{2,1,0:T(1,128)} %row_in.1, s32[1,1,3]{2,1,0:T(1,128)} %col_in.1, ...), custom_call_target="tpu_custom_call" | custom-call | tf_op jit(solution)/shard_map/ptycho/pallas_call | solution.py:606
  71.3 2.0 %scale.1 = (f32[4,2,192,128]{3,2,1,0:T(8,128)}, f32[1,4,8,256]{3,2,1,0:T(8,128)}) custom-call(f32[4,2,192,128]{3,2,1,0:T(8,128)} %get-tuple-element.5.obj, f32[1,4,8,256]{3,2,1,0:T(8,128)} %get-tuple-element.6.pgrad, f32[8,128]{1,0:T(8,128)} %get-tuple-element.7.scale), custom_call_target="tpu_custom_call" | custom-call | tf_op jit(solution)/shard_map/scale/pallas_call | solution.py:630

commit v4 on v3

--- a/solution.py
+++ b/solution.py
@@ -61,11 +61,11 @@
 
 
 def kernel(
-    pot, probe, amps_in, row_in, col_in, cnt_in, fwd_hbm, inv_hbm, kern_hbm,
+    pot, probe, amps_in, row_hbm, col_hbm, cnt_hbm, fwd_hbm, inv_hbm, kern_hbm,
     out_obj, out_probe, out_scale,
     n0, n1, n2, n3, c0, c1, c2, c3, gn, gc, rbuf, xbuf, sbuf, amps, amps_out, metav, meta_out, meta,
     pbuf, psi, wav, tr, gp, pgr, px, pzr, pown, pfin,
-    mis, misr, smis, stage, chunk, stage_sem, amps_raw, fwd_in, inv_in, kern_in,
+    mis, misr, smis, stage, chunk, stage_sem, amps_raw, fwd_in, inv_in, kern_in, row_in, col_in, cnt_in,
     loc_sem, s_misc, r_probe, r_meta, r_amp,
     s_n, r_n, s_c, r_c, s_f, r_f, s_pz, r_pz, s_pf, r_pf,
     s_x, r_x, s_r, r_r, s_rn, r_rn, s_px, r_px, s_pq, r_pq, s_po, r_po, s_m, r_m,
@@ -112,23 +112,28 @@
 
     own_pot = [pltpu.make_async_copy(pot.at[s], stage.at[s], stage_sem.at[s]) for s in range(SLICES)]
     own_p = pltpu.make_async_copy(probe.at[0], chunk, stage_sem.at[4])
+    scalars = [pltpu.make_async_copy(src, dst, stage_sem.at[9 + i]) for i, (src, dst) in enumerate(((row_hbm, row_in), (col_hbm, col_in), (cnt_hbm, cnt_in)))]
+    for q in scalars:
+        q.start()
     own_p.start()
     for s in range(SLICES):
         own_pot[s].start()
 
+    own_a = pltpu.make_async_copy(amps_in.at[0, 0], amps_raw, stage_sem.at[5])
+    consts = [pltpu.make_async_copy(src, dst, stage_sem.at[6 + i]) for i, (src, dst) in enumerate(((fwd_hbm, fwd_in), (inv_hbm, inv_in), (kern_hbm, kern_in)))]
+    own_a.start()
+    for q in consts:
+        q.start()
+
     lane = lax.broadcasted_iota(jnp.int32, (8, N), 1)
     packed = jnp.zeros((8, N), jnp.int32)
+    for q in scalars:
+        q.wait()
     for p in range(SLOTS):
         packed = jnp.where(lane == p, row_in[0, 0, p], packed)
         packed = jnp.where(lane == SLOTS + p, col_in[0, 0, p], packed)
     packed = jnp.where(lane == 2 * SLOTS, cnt_in[0, 0], packed)
     meta_out[...] = packed
-    own_a = pltpu.make_async_copy(amps_in.at[0, 0], amps_raw, stage_sem.at[5])
-    consts = [pltpu.make_async_copy(src, dst, stage_sem.at[6 + i]) for i, (src, dst) in enumerate(((fwd_hbm, fwd_in), (inv_hbm, inv_in), (kern_hbm, kern_in)))]
-    own_a.start()
-    for q in consts:
-        q.start()
-
     pl.semaphore_wait(barrier, len(partners))
 
     def half_of(ref, hh):
@@ -444,7 +449,7 @@
         def _():
             send_rn[s].start()
 
-    def back(s):
+    def back(s, first, last):
         def one(p, carry):
             t = trans_at(s, p)
             kern = pair(kern_in)
@@ -454,7 +459,7 @@
                 put(wav, waves[m], p, m)
             return carry
 
-        lax.fori_loop(0, SLOTS, one, 0, unroll=True)
+        lax.fori_loop(first, last, one, 0, unroll=True)
 
     def hand_over(s):
         give_x[s].wait_recv()
@@ -463,11 +468,13 @@
 
     for s in reversed(range(1, SLICES)):
         patch_grad(s)
-        back(s)
-        hand_over(s)
-        if s == 2:
-            take_mis(0)
-            send_mis(1)
+        if s == SLICES - 1:
+            back(s, 0, 2)
+            hand_over(s)
+            back(s, 2, SLOTS)
+        else:
+            back(s, 0, SLOTS)
+            hand_over(s)
 
     pgr[...] = jnp.zeros_like(pgr)
 
@@ -481,6 +488,8 @@
     lax.fori_loop(0, SLOTS, probe_slot, 0)
     give_p = remote(half_of(pgr, oc), px, s_px, r_px, sibling)
     give_p.start()
+    take_mis(0)
+    send_mis(1)
     patch_grad(0)
     give_p.wait_recv()
     px[...] = px[...] + pgr[:, :, pl.ds(pl.multiple_of(c * 8, 8), 8), :]
@@ -593,7 +602,6 @@
     forward, inverse = tables()
     kern = propagator()
     vmem = pl.BlockSpec(memory_space=pltpu.VMEM)
-    smem = pl.BlockSpec(memory_space=pltpu.SMEM)
     hbm = pl.BlockSpec(memory_space=pltpu.HBM)
     dma = pltpu.SemaphoreType.DMA
     tile = (SLICES, 2, ROWS, N)
@@ -606,7 +614,7 @@
     obj, pgrad, scale = pl.pallas_call(
         kernel,
         out_shape=tuple(jax.ShapeDtypeStruct(shape, F32) for shape in (tile, (1, *chunk), (8, N))),
-        in_specs=[hbm, hbm, hbm, smem, smem, smem, hbm, hbm, hbm],
+        in_specs=[hbm] * 9,
         out_specs=(hbm, vmem, vmem),
         scratch_shapes=[
             *[f32(*tile[1:])] * 8, f32(*tile), f32(*tile), f32(*tile),
@@ -616,8 +624,9 @@
             f32(MODES, ZS, 16, 2 * N), f32(SLICES - 1, SLOTS, *wave), f32(SLOTS, *wave),
             f32(SLICES, SLOTS, 2, N, N), f32(2, 256, N),
             f32(MODES, ZS, 16, 2 * N), f32(MODES, ZS, 8, 2 * N), f32(ZS - 1, *chunk), f32(*chunk), f32(*chunk),
-            f32(16, N), f32(3, 7, 16, N), f32(3, 16, N), f32(*tile), f32(*chunk), dma((9,)),
+            f32(16, N), f32(3, 7, 16, N), f32(3, 16, N), f32(*tile), f32(*chunk), dma((12,)),
             pltpu.VMEM((SLOTS, N, N), BF16), pltpu.VMEM((2 * N, 2 * N), BF16), pltpu.VMEM((2 * N, 2 * N), BF16), f32(N, 2 * N),
+            pltpu.SMEM((1, 1, SLOTS), jnp.int32), pltpu.SMEM((1, 1, SLOTS), jnp.int32), pltpu.SMEM((1, 1), jnp.int32),
             dma((8,)), dma((3,)), dma, dma, dma,
             dma((4,)), dma((4,)), dma((4, 2)), dma((4,)), dma((4,)), dma((4,)),
             dma((7,)), dma((7,)), dma, dma,

time: 73.6 us -> 72.9 us (level)
  no operation moved by 1% of the time
where the time goes in v4:
time: 72.9 us; the launch traced here: 72.7 us
  Pallas kernels  71.3 us (98%)
  between operations  1.45 us (2%)
    pallas_call x1, Pallas kernels, body(): pl.pallas_call(kernel, out_shape=tuple((jax.ShapeDtypeStruct(shape, F32)...  69.3 us
    pallas_call x1, Pallas kernels, body(): pl.pallas_call(finish, out_shape=tuple((jax.ShapeDtypeStruct(shape, F32)...  2.01 us

profile of v4, /device:TPU:1, one launch (start us, length us, event | category | flops | bytes accessed | tf_op | source)
XLA Modules:
  0.0 72.7 jit_solution(12471388838739063358)
XLA Ops:
  1.3 69.3 %ptycho.1 = (f32[4,2,192,128]{3,2,1,0:T(8,128)}, f32[1,4,8,256]{3,2,1,0:T(8,128)}, f32[8,128]{1,0:T(8,128)}) custom-call(f32[4,2,192,128]{3,2,1,0:T(8,128)} %pot.1, f32[1,4,8,256]{3,2,1,0:T(8,128)} %probe.1, bf16[1,1,3,128,128]{4,3,2,1,0:T(8,128)(2,1)} %amps_in.1, s32[1,1,3]{2,1,0:T(1,128)} %row_hbm.1, s32[1,1,3]{2,1,0:T(1,128)} %col_hbm.1, ...), custom_call_target="tpu_custom_call" | custom-call | tf_op jit(solution)/shard_map/ptycho/pallas_call | solution.py:614
  70.6 2.0 %scale.1 = (f32[4,2,192,128]{3,2,1,0:T(8,128)}, f32[1,4,8,256]{3,2,1,0:T(8,128)}) custom-call(f32[4,2,192,128]{3,2,1,0:T(8,128)} %get-tuple-element.5.obj, f32[1,4,8,256]{3,2,1,0:T(8,128)} %get-tuple-element.6.pgrad, f32[8,128]{1,0:T(8,128)} %get-tuple-element.7.scale), custom_call_target="tpu_custom_call" | custom-call | tf_op jit(solution)/shard_map/scale/pallas_call | solution.py:639

commit v5 on v4

--- a/solution.py
+++ b/solution.py
@@ -64,7 +64,7 @@
     pot, probe, amps_in, row_hbm, col_hbm, cnt_hbm, fwd_hbm, inv_hbm, kern_hbm,
     out_obj, out_probe, out_scale,
     n0, n1, n2, n3, c0, c1, c2, c3, gn, gc, rbuf, xbuf, sbuf, amps, amps_out, metav, meta_out, meta,
-    pbuf, psi, wav, tr, gp, pgr, px, pzr, pown, pfin,
+    pbuf, psi, wav0, wav1, tr, gp, pgr, px, pzr, pown, pfin,
     mis, misr, smis, stage, chunk, stage_sem, amps_raw, fwd_in, inv_in, kern_in, row_in, col_in, cnt_in,
     loc_sem, s_misc, r_probe, r_meta, r_amp,
     s_n, r_n, s_c, r_c, s_f, r_f, s_pz, r_pz, s_pf, r_pf,
@@ -361,6 +361,9 @@
     mis[0:8, :] = jnp.zeros((8, N), F32)
     mis[8:16, :] = jnp.zeros((8, N), F32) + count.astype(F32)
 
+    wavs = (wav0, wav1)
+    wav = wavs[(SLICES - 1) % 2]
+
     def spectrum(p, carry):
         t = trans_at(SLICES - 1, p)
         far = dft([cmul(t, psi_at(SLICES - 1, p, m)) for m in range(MODES)], fwd_in[...], inv_in[...])
@@ -430,7 +433,7 @@
 
         def one(p, carry):
             t = trans_at(s, p)
-            parts = [cmulc(psi_at(s, p, m), pair(wav, p, m)) for m in range(MODES)]
+            parts = [cmulc(psi_at(s, p, m), pair(wavs[s % 2], p, m)) for m in range(MODES)]
             tg = (parts[0][0] + parts[1][0] + parts[2][0] + parts[3][0], parts[0][1] + parts[1][1] + parts[2][1] + parts[3][1])
             q = cmulc(t, tg)
             in_n, in_c, col = masks(p, ROWS)
@@ -453,10 +456,10 @@
         def one(p, carry):
             t = trans_at(s, p)
             kern = pair(kern_in)
-            waves = dft([cmulc(t, pair(wav, p, m)) for m in range(MODES)], fwd_in[...], inv_in[...])
+            waves = dft([cmulc(t, pair(wavs[s % 2], p, m)) for m in range(MODES)], fwd_in[...], inv_in[...])
             waves = dft([cmulc(kern, w) for w in waves], inv_in[...], fwd_in[...])
             for m in range(MODES):
-                put(wav, waves[m], p, m)
+                put(wavs[(s - 1) % 2], waves[m], p, m)
             return carry
 
         lax.fori_loop(first, last, one, 0, unroll=True)
@@ -467,13 +470,15 @@
         send_r[s].start()
 
     for s in reversed(range(1, SLICES)):
-        patch_grad(s)
+        if s > 1:
+            patch_grad(s)
         if s == SLICES - 1:
             back(s, 0, 2)
             hand_over(s)
             back(s, 2, SLOTS)
         else:
             back(s, 0, SLOTS)
+        if s == 2:
             hand_over(s)
 
     pgr[...] = jnp.zeros_like(pgr)
@@ -481,13 +486,14 @@
     def probe_slot(p, carry):
         t = trans_at(0, p)
         for m in range(MODES):
-            w = jnp.concatenate(cmulc(t, pair(wav, p, m)), 1)
+            w = jnp.concatenate(cmulc(t, pair(wavs[0], p, m)), 1)
             pgr[m] = pgr[m] + w.reshape(ZS, 16, 2 * N)
         return carry
 
     lax.fori_loop(0, SLOTS, probe_slot, 0)
     give_p = remote(half_of(pgr, oc), px, s_px, r_px, sibling)
     give_p.start()
+    patch_grad(1)
     take_mis(0)
     send_mis(1)
     patch_grad(0)
@@ -501,6 +507,7 @@
     def _():
         send_rn[0].start()
 
+    hand_over(1)
     hand_over(0)
     take_mis(1)
     send_mis(2)
@@ -621,7 +628,7 @@
             f32(SLICES, ROWS, N), f32(SLICES, ROWS, N),
             f32(SLOTS, N, N), f32(SLOTS, N, N),
             pltpu.VMEM((8, N), jnp.int32), pltpu.VMEM((8, N), jnp.int32), pltpu.SMEM((8, N), jnp.int32),
-            f32(MODES, ZS, 16, 2 * N), f32(SLICES - 1, SLOTS, *wave), f32(SLOTS, *wave),
+            f32(MODES, ZS, 16, 2 * N), f32(SLICES - 1, SLOTS, *wave), f32(SLOTS, *wave), f32(SLOTS, *wave),
             f32(SLICES, SLOTS, 2, N, N), f32(2, 256, N),
             f32(MODES, ZS, 16, 2 * N), f32(MODES, ZS, 8, 2 * N), f32(ZS - 1, *chunk), f32(*chunk), f32(*chunk),
             f32(16, N), f32(3, 7, 16, N), f32(3, 16, N), f32(*tile), f32(*chunk), dma((12,)),

time: 72.9 us -> 72.5 us (level)
  no operation moved by 1% of the time
where the time goes in v5:
time: 72.5 us; the launch traced here: 72.4 us
  Pallas kernels  71 us (98%)
  between operations  1.45 us (2%)
    pallas_call x1, Pallas kernels, body(): pl.pallas_call(kernel, out_shape=tuple((jax.ShapeDtypeStruct(shape, F32)...  69 us
    pallas_call x1, Pallas kernels, body(): pl.pallas_call(finish, out_shape=tuple((jax.ShapeDtypeStruct(shape, F32)...  2.01 us

profile of v5, /device:TPU:1, one launch (start us, length us, event | category | flops | bytes accessed | tf_op | source)
XLA Modules:
  0.0 72.4 jit_solution(8389303683088514259)
XLA Ops:
  1.3 69.0 %ptycho.1 = (f32[4,2,192,128]{3,2,1,0:T(8,128)}, f32[1,4,8,256]{3,2,1,0:T(8,128)}, f32[8,128]{1,0:T(8,128)}) custom-call(f32[4,2,192,128]{3,2,1,0:T(8,128)} %pot.1, f32[1,4,8,256]{3,2,1,0:T(8,128)} %probe.1, bf16[1,1,3,128,128]{4,3,2,1,0:T(8,128)(2,1)} %amps_in.1, s32[1,1,3]{2,1,0:T(1,128)} %row_hbm.1, s32[1,1,3]{2,1,0:T(1,128)} %col_hbm.1, ...), custom_call_target="tpu_custom_call" | custom-call | tf_op jit(solution)/shard_map/ptycho/pallas_call | solution.py:621
  70.2 2.0 %scale.1 = (f32[4,2,192,128]{3,2,1,0:T(8,128)}, f32[1,4,8,256]{3,2,1,0:T(8,128)}) custom-call(f32[4,2,192,128]{3,2,1,0:T(8,128)} %get-tuple-element.5.obj, f32[1,4,8,256]{3,2,1,0:T(8,128)} %get-tuple-element.6.pgrad, f32[8,128]{1,0:T(8,128)} %get-tuple-element.7.scale), custom_call_target="tpu_custom_call" | custom-call | tf_op jit(solution)/shard_map/scale/pallas_call | solution.py:646
